TPU v7x, 32 devices: a whole 2x2x4 slice. The times are simulated.
32 devices in a mesh: groups: 2 (over y), rows: 4 (over z), cols: 2 (over x), sub: 2 (over core).
Axes of the slice: x: 2, y: 2, z: 4, core: 2. Of those that a mesh axis runs over, the one named last changes fastest.
Arguments:
- features: bfloat16 [128, 256, 512], P(None, ('groups', 'rows'), ('cols', 'sub')), parts along dimension 1, may hold values from -9 to 9
- guide_image: bfloat16 [3, 256, 512], P(None, ('groups', 'rows'), ('cols', 'sub')), parts along dimension 1, may hold values from 0 to 1
- conv_weight: bfloat16 [3, 3, 64, 128], replicated, may hold values from -0.1875 to 0.1875
- head_weight: float32 [2, 64], replicated, may hold values from -0.75 to 0.75
- pixel_mask: int32 [256, 512], P(('groups', 'rows', 'cols', 'sub')), parts along dimension 0, may hold values 0 or 1
Outputs:
- mixture: float32 [256, 512], P(('groups', 'rows', 'cols', 'sub')), parts along dimension 0
There are 2 independent parts, one for each index of `groups`. A program takes and returns all parts, laid end to end along the dimension named above; an argument that names none is the same for every part. Nothing has to cross between parts.
All inputs are finite; a program needn't handle non-finite values. No bound on the sum of `pixel_mask` on one device may be relied on, other than what follows from the above.
Results may differ from a plain program's by a relative error of at most 0.0003.
Values may be sent and summed in bfloat16 or wider, within the bound.
A program may use at most 64 MiB of HBM per device.

v0:
```python
import jax
import jax.numpy as jnp
from jax import lax
from jax.sharding import PartitionSpec as P

ITERS = 2
RIDGE = 0.05
BASE_WEIGHT = 0.1


def with_halo(cells, sides, width):
    for axis, dim in sides:
        count = lax.axis_size(axis)
        ends = count - 1
        head = lax.slice_in_dim(cells, 0, width, axis=dim)
        tail = lax.slice_in_dim(cells, cells.shape[dim] - width, cells.shape[dim], axis=dim)
        cells = jnp.concatenate(
            [
                lax.ppermute(tail, axis, [(i, (i + 1) % count) for i in range(ends)]),
                cells,
                lax.ppermute(head, axis, [((i + 1) % count, i) for i in range(ends)]),
            ],
            axis=dim,
        )
    return cells


def box_sum(extended):
    vertical = extended[:, :-2, :] + extended[:, 1:-1, :] + extended[:, 2:, :]
    return vertical[:, :, :-2] + vertical[:, :, 1:-1] + vertical[:, :, 2:]


def window_stats(guide_ext):
    average = box_sum(guide_ext) / 9.0
    red_ext, green_ext, blue_ext = (guide_ext[0], guide_ext[1], guide_ext[2])
    products = jnp.stack(
        [
            red_ext * red_ext,
            red_ext * green_ext,
            red_ext * blue_ext,
            green_ext * green_ext,
            green_ext * blue_ext,
            blue_ext * blue_ext,
        ]
    )
    second = box_sum(products) / 9.0
    cov_rr = second[0] - average[0] * average[0] + RIDGE
    cov_rg = second[1] - average[0] * average[1]
    joint_spread_redyellow = second[2] - average[0] * average[2]
    cov_gg = second[3] - average[1] * average[1] + RIDGE
    covariance_green_blue = second[4] - average[1] * average[2]
    cov_bb = second[5] - average[2] * average[2] + RIDGE
    cof_rr = cov_gg * cov_bb - covariance_green_blue * covariance_green_blue
    cof_rg = joint_spread_redyellow * covariance_green_blue - cov_rg * cov_bb
    cof_rb = cov_rg * covariance_green_blue - joint_spread_redyellow * cov_gg
    cof_gg = cov_rr * cov_bb - joint_spread_redyellow * joint_spread_redyellow
    cofactor_green_blue = cov_rg * joint_spread_redyellow - cov_rr * covariance_green_blue
    cof_bb = cov_rr * cov_gg - cov_rg * cov_rg
    determinant = cov_rr * cof_rr + cov_rg * cof_rg + joint_spread_redyellow * cof_rb
    inverse = jnp.stack([cof_rr, cof_rg, cof_rb, cof_gg, cofactor_green_blue, cof_bb]) / determinant
    return (average, inverse)


def coefficients(field_ext, guide_ext, average, inverse):
    field_box = box_sum(field_ext)[0] / 9.0
    crossed = box_sum(guide_ext * field_ext) / 9.0 - average * field_box
    slope_r = inverse[0] * crossed[0] + inverse[1] * crossed[1] + inverse[2] * crossed[2]
    slope_g = inverse[1] * crossed[0] + inverse[3] * crossed[1] + inverse[4] * crossed[2]
    gradient_coefficient_third = (
        inverse[2] * crossed[0] + inverse[4] * crossed[1] + inverse[5] * crossed[2]
    )
    offset = field_box - (
        slope_r * average[0] + slope_g * average[1] + gradient_coefficient_third * average[2]
    )
    return jnp.stack([slope_r, slope_g, gradient_coefficient_third, offset])


def apply_operator(field_map, coef_ext, guide_local_tile, weights):
    summed = box_sum(coef_ext)
    smooth = (
        summed[0] * guide_local_tile[0]
        + summed[1] * guide_local_tile[1]
        + summed[2] * guide_local_tile[2]
        + summed[3]
    )
    return 9.0 * field_map - smooth + weights * field_map


def head_maps(extended, conv_weight, head_weight, height, columns):
    channels = extended.shape[0]
    accumulated = jnp.zeros((conv_weight.shape[2], height * columns), jnp.float32)
    for shift_r in range(3):
        for shift_c in range(3):
            window_cell_count = extended[
                :, shift_r : shift_r + height, shift_c : shift_c + columns
            ].reshape(channels, height * columns)
            accumulated = accumulated + jnp.dot(
                conv_weight[shift_r, shift_c], window_cell_count, preferred_element_type=jnp.float32
            )
    hidden = jnp.maximum(accumulated, 0.0)
    logits = jnp.dot(head_weight, hidden, precision=lax.Precision.HIGHEST)
    seed_map = jax.nn.sigmoid(logits[0])
    certainty = jax.nn.softplus(logits[1])
    return jnp.stack([seed_map, certainty]).reshape(2, height, columns)


def pad_columns(stack):
    return jnp.pad(stack, ((0, 0), (0, 0), (1, 1)))


def strip_rim(stack):
    return pad_columns(with_halo(stack, ((("rows", "cols", "sub"), 1),), 1))


def global_sums(values):
    return lax.psum((values[0], values[1]), ("rows", "cols", "sub"))


def on_device(features, guide_image, conv_weight, head_weight, pixel_mask):
    tile_rows, tile_cols = (features.shape[1], features.shape[2])
    outgoing = (features, guide_image)
    rimmed = (
        with_halo(outgoing[0], (("rows", 1), (("cols", "sub"), 2)), 1),
        with_halo(outgoing[1], (("rows", 1), (("cols", "sub"), 2)), 1),
    )
    predictor_result = head_maps(rimmed[0], conv_weight, head_weight, tile_rows, tile_cols)
    guide_float = guide_image.astype(jnp.float32)
    tile_average, tile_inverse_matrix = window_stats(rimmed[1].astype(jnp.float32))
    stacked = jnp.concatenate([predictor_result, guide_float, tile_average, tile_inverse_matrix])
    strips = lax.all_to_all(stacked, ("cols", "sub"), split_axis=1, concat_axis=2, tiled=True)
    seed_map = strips[0]
    certainty = strips[1]
    guide_local_tile = strips[2:5]
    guide_ext = strip_rim(guide_local_tile)
    average, inverse = (strips[5:8], strips[8:14])
    weights = BASE_WEIGHT + pixel_mask.astype(jnp.float32) * certainty

    def operate(field_map):
        field_ext = strip_rim(field_map[None])
        coef = coefficients(field_ext, guide_ext, average, inverse)
        coef_ext = strip_rim(coef)
        return apply_operator(field_map, coef_ext, guide_local_tile, weights)

    mixture = seed_map
    residual = weights * seed_map - operate(seed_map)
    image_dir = operate(residual)
    norm_now, product = global_sums((jnp.sum(residual * residual), jnp.sum(residual * image_dir)))
    step_size = norm_now / product
    direction, along = (residual, image_dir)
    for iteration in range(ITERS):
        mixture = mixture + step_size * direction
        residual = residual - step_size * along
        if iteration + 1 < ITERS:
            image_dir = operate(residual)
            norm_next, product = global_sums(
                (jnp.sum(residual * residual), jnp.sum(residual * image_dir))
            )
            ratio = norm_next / norm_now
            step_size = norm_next / (product - ratio * norm_next / step_size)
            direction = residual + ratio * direction
            along = image_dir + ratio * along
            norm_now = norm_next
    return mixture


def solution(mesh):
    return jax.shard_map(
        on_device,
        mesh=mesh,
        in_specs=(
            P(None, ("groups", "rows"), ("cols", "sub")),
            P(None, ("groups", "rows"), ("cols", "sub")),
            P(),
            P(),
            P(("groups", "rows", "cols", "sub"), None),
        ),
        out_specs=P(("groups", "rows", "cols", "sub"), None),
        check_vma=False,
    )
```

profile of v0, /device:TPU:0, one launch (start us, length us, event | category | flops | bytes accessed | tf_op | source)
XLA Modules:
  0.0 178.0 jit_solution(652070751891009587)
XLA Ops:
  0.0 0.8 fusion.96
  0.8 4.9 %collective-permute-start.4 = (bf16[3,1,128]{2,1,0:T(2,128)(2,1)S(1)}, bf16[3,1,128]{2,1,0:T(2,128)(2,1)S(1)}, u32[]{:S(2)}, u32[]{:S(2)}) collective-permute-start(bf16[3,1,128]{2,1,0:T(2,128)(2,1)S(1)} %get-tuple-element.77), channel_id=1, source_target_pairs={{0,4},{4,8},{8,12},{1,5},{5,9},{9,13},{2,6},{6,10},{10,14},{3,7},{... | collective-permute-start | bytes 2312 | tf_op jit(solution)/shard_map/ppermute | solution.py:19
  5.7 1.3 collective-permute-start.5
  7.0 2.5 %copy.68 = bf16[128,32,128]{0,1,2:T(8,128)(2,1)S(1)} copy(bf16[128,32,128]{2,1,0:T(8,128)(2,1)} %param.5) | data formatting | bytes 2097152 | tf_op args[0]
  9.6 1.6 collective-permute-done.5
  11.3 1.3 collective-permute-start.6
  12.6 1.3 collective-permute-start.7
  13.9 4.1 %collective-permute-start = (bf16[128,1,128]{0,1,2:T(2,128)(2,1)S(1)}, bf16[128,1,128]{0,1,2:T(2,128)(2,1)}, u32[]{:S(2)}, u32[]{:S(2)}) collective-permute-start(bf16[128,1,128]{0,1,2:T(2,128)(2,1)S(1)} %get-tuple-element.47), channel_id=1, source_target_pairs={{0,4},{4,8},{8,12},{1,5},{5,9},{9,13},{2,6},{6,10},{10,14},{3,7},{... | collective-permute-start | bytes 98312 | tf_op jit(solution)/shard_map/ppermute | solution.py:19
  18.0 1.3 collective-permute-start.1
  19.7 4.5 %collective-permute-done.1 = bf16[128,1,128]{0,1,2:T(2,128)(2,1)} collective-permute-done((bf16[128,1,128]{0,1,2:T(2,128)(2,1)S(1)}, bf16[128,1,128]{0,1,2:T(2,128)(2,1)}, u32[]{:S(2)}, u32[]{:S(2)}) %collective-permute-start.1) | collective-permute-done | bytes 32800 | tf_op jit(solution)/shard_map/ppermute | solution.py:21
  24.2 1.6 pad_maximum_fusion
  26.8 3.9 %collective-permute-start.2 = (bf16[128,34,1]{0,1,2:T(8,128)(2,1)}, bf16[128,34,1]{0,1,2:T(8,128)(2,1)}, u32[]{:S(2)}, u32[]{:S(2)}) collective-permute-start(bf16[128,34,1]{0,1,2:T(8,128)(2,1)} %get-tuple-element.37), channel_id=1, source_target_pairs={{0,1},{1,2},{2,3},{4,5},{5,6},{6,7},{8,9},{9,10},{10,11},{12,13},{... | collective-permute-start | bytes 26120 | tf_op jit(solution)/shard_map/ppermute | solution.py:19
  30.7 1.3 collective-permute-start.3
  32.0 1.6 copy.73
  33.6 1.6 copy.76
  35.2 2.1 %pad_maximum_fusion.3 = (bf16[128,32,128]{2,1,0:T(8,128)(2,1)S(1)}, bf16[128,32,128]{2,1,0:T(8,128)(2,1)S(1)}) fusion(bf16[128,32,128]{2,1,0:T(8,128)(2,1)S(1)} %copy-done.1, bf16[128,1,128]{2,1,0:T(2,128)(2,1)} %copy.73, bf16[128,1,128]{2,1,0:T(2,128)(2,1)} %copy.76), kind=kLoop, calls=%fused_computation.30 | loop fusion | flops 4194304 | bytes 3211264 | tf_op jit(solution)/shard_map/concatenate | solution.py:17
  37.8 0.7 copy.71
  38.6 0.8 fusion.6
  39.9 0.7 constant_dynamic-update-slice_fusion
  40.6 0.8 fusion.90
  44.4 0.8 fusion.4
  45.1 0.7 convolution_bitcast_fusion.4
  46.4 12.0 %all_to_all.15 = f32[14,32,128]{2,0,1:T(8,128)S(1)} all-to-all(f32[14,32,128]{2,0,1:T(8,128)S(1)} %copy.77), channel_id=1, replica_groups=mesh['groups'=2,'rows'=4,'cols'=2,'sub'=2] {'cols','sub'}, dimensions={1} | all-to-all | bytes 458752 | tf_op jit(solution)/shard_map/all_to_all | solution.py:130
  58.6 1.4 collective-permute-start.10
  60.0 1.3 collective-permute-start.11
  61.3 3.5 %collective-permute-start.8 = (f32[3,1,512]{2,1,0:T(1,128)S(1)}, f32[3,1,512]{2,1,0:T(1,128)S(1)}, u32[]{:S(2)}, u32[]{:S(2)}) collective-permute-start(f32[3,1,512]{2,1,0:T(1,128)S(1)} %get-tuple-element.71), channel_id=1, source_target_pairs={{0,1},{1,2},{2,3},{3,4},{4,5},{5,6},{6,7},{7,8},{8,9},{9,10},{10,1... | collective-permute-start | bytes 18440 | tf_op jit(solution)/shard_map/ppermute | solution.py:19
  64.8 1.3 collective-permute-start.9
  66.4 2.8 %collective-permute-done.9 = f32[3,1,512]{2,1,0:T(1,128)S(1)} collective-permute-done((f32[3,1,512]{2,1,0:T(1,128)S(1)}, f32[3,1,512]{2,1,0:T(1,128)S(1)}, u32[]{:S(2)}, u32[]{:S(2)}) %collective-permute-start.9) | collective-permute-done | bytes 6176 | tf_op jit(solution)/shard_map/ppermute | solution.py:21
  69.5 4.3 %collective-permute-start.12 = (f32[4,1,512]{2,1,0:T(1,128)S(1)}, f32[4,1,512]{2,1,0:T(1,128)S(1)}, u32[]{:S(2)}, u32[]{:S(2)}) collective-permute-start(f32[4,1,512]{2,1,0:T(1,128)S(1)} %get-tuple-element.69), channel_id=1, source_target_pairs={{0,1},{1,2},{2,3},{3,4},{4,5},{5,6},{6,7},{7,8},{8,9},{9,10},{10,1... | collective-permute-start | bytes 24584 | tf_op jit(solution)/shard_map/ppermute | solution.py:19
  73.8 1.3 collective-permute-start.13
  75.1 2.0 %collective-permute-done.13 = f32[4,1,512]{2,1,0:T(1,128)S(1)} collective-permute-done((f32[4,1,512]{2,1,0:T(1,128)S(1)}, f32[4,1,512]{2,1,0:T(1,128)S(1)}, u32[]{:S(2)}, u32[]{:S(2)}) %collective-permute-start.13) | collective-permute-done | bytes 8224 | tf_op jit(solution)/shard_map/ppermute | solution.py:21
  77.4 5.9 %collective-permute-start.14 = (f32[1,1,512]{2,1,0:T(1,128)S(1)}, f32[1,1,512]{2,1,0:T(1,128)S(1)}, u32[]{:S(2)}, u32[]{:S(2)}) collective-permute-start(f32[1,1,512]{2,1,0:T(1,128)S(1)} %get-tuple-element.87), channel_id=1, source_target_pairs={{0,1},{1,2},{2,3},{3,4},{4,5},{5,6},{6,7},{7,8},{8,9},{9,10},{10,1... | collective-permute-start | bytes 6152 | tf_op jit(solution)/shard_map/ppermute | solution.py:19
  83.3 1.3 collective-permute-start.15
  84.6 1.7 collective-permute-done.15
  86.9 4.7 %collective-permute-start.16 = (f32[4,1,512]{2,1,0:T(1,128)S(1)}, f32[4,1,512]{2,1,0:T(1,128)S(1)}, u32[]{:S(2)}, u32[]{:S(2)}) collective-permute-start(f32[4,1,512]{2,1,0:T(1,128)S(1)} %get-tuple-element.67), channel_id=1, source_target_pairs={{0,1},{1,2},{2,3},{3,4},{4,5},{5,6},{6,7},{7,8},{8,9},{9,10},{10,1... | collective-permute-start | bytes 24584 | tf_op jit(solution)/shard_map/ppermute | solution.py:19
  91.6 1.3 collective-permute-start.17
  92.9 1.8 collective-permute-done.17
  94.9 0.6 multiply_reduce_fusion.1
  95.6 33.0 %all-reduce.8 = (f32[]{:T(128)}, f32[]{:T(128)}) all-reduce(f32[]{:T(128)} %get-tuple-element.8, f32[]{:T(128)} %get-tuple-element.7), channel_id=1, replica_groups=mesh['groups'=2,'rows'=4,'cols'=2,'sub'=2] {'rows','cols','sub'}, use_global_device_ids=true, to_apply=%region_1.2 | all-reduce | flops 2 | bytes 16 | tf_op jit(solution)/shard_map/psum | solution.py:116
  129.9 1.3 collective-permute-start.18
  131.2 1.3 collective-permute-start.19
  132.5 1.7 collective-permute-done.19
  134.8 2.1 %collective-permute-start.20 = (f32[4,1,512]{2,1,0:T(1,128)S(1)}, f32[4,1,512]{2,1,0:T(1,128)S(1)}, u32[]{:S(2)}, u32[]{:S(2)}) collective-permute-start(f32[4,1,512]{2,1,0:T(1,128)S(1)} %get-tuple-element.65), channel_id=1, source_target_pairs={{0,1},{1,2},{2,3},{3,4},{4,5},{5,6},{6,7},{7,8},{8,9},{9,10},{10,1... | collective-permute-start | bytes 24584 | tf_op jit(solution)/shard_map/ppermute | solution.py:19
  136.9 1.3 collective-permute-start.21
  138.2 1.8 collective-permute-done.21
  140.3 0.6 fusion.29
  140.9 32.0 %all-reduce.7 = (f32[]{:T(128)}, f32[]{:T(128)}) all-reduce(f32[]{:T(128)} %get-tuple-element.6, f32[]{:T(128)} %get-tuple-element.5), channel_id=1, replica_groups=mesh['groups'=2,'rows'=4,'cols'=2,'sub'=2] {'rows','cols','sub'}, use_global_device_ids=true, to_apply=%region_5.6 | all-reduce | flops 2 | bytes 16 | tf_op jit(solution)/shard_map/psum | solution.py:116
  177.4 0.6 multiply_add_fusion
  (105 shorter events, 8.5 us)
Async XLA Ops:
  0.0 45.1 %copy-start = (f32[2,64]{1,0:T(2,128)S(1)}, f32[2,64]{1,0:T(2,128)}, u32[]{:S(2)}) copy-start(f32[2,64]{1,0:T(2,128)} %param.8) | copy-start | bytes 1540
  0.0 11.2 %copy-start.2 = (bf16[3,32,128]{2,1,0:T(8,128)(2,1)S(1)}, bf16[3,32,128]{2,1,0:T(8,128)(2,1)}, u32[]{:S(2)}) copy-start(bf16[3,32,128]{2,1,0:T(8,128)(2,1)} %param.6) | copy-start | bytes 73732
  0.8 8.8 %collective-permute-start.4 = (bf16[3,1,128]{2,1,0:T(2,128)(2,1)S(1)}, bf16[3,1,128]{2,1,0:T(2,128)(2,1)S(1)}, u32[]{:S(2)}, u32[]{:S(2)}) collective-permute-start(bf16[3,1,128]{2,1,0:T(2,128)(2,1)S(1)} %get-tuple-element.77), channel_id=1, source_target_pairs={{0,4},{4,8},{8,12},{1,5},{5,9},{9,13},{2,6},{6,10},{10,14},{3,7},{... | collective-permute-start | bytes 2312 | tf_op jit(solution)/shard_map/ppermute | solution.py:19
  5.7 5.5 %collective-permute-start.5 = (bf16[3,1,128]{2,1,0:T(2,128)(2,1)S(1)}, bf16[3,1,128]{2,1,0:T(2,128)(2,1)S(1)}, u32[]{:S(2)}, u32[]{:S(2)}) collective-permute-start(bf16[3,1,128]{2,1,0:T(2,128)(2,1)S(1)} %get-tuple-element.78), channel_id=1, source_target_pairs={{4,0},{8,4},{12,8},{5,1},{9,5},{13,9},{6,2},{10,6},{14,10},{7,3},{... | collective-permute-start | bytes 2312 | tf_op jit(solution)/shard_map/ppermute | solution.py:21
  11.3 8.0 %collective-permute-start.6 = (bf16[3,34,1]{2,1,0:T(8,128)(2,1)S(1)}, bf16[3,34,1]{2,1,0:T(8,128)(2,1)S(1)}, u32[]{:S(2)}, u32[]{:S(2)}) collective-permute-start(bf16[3,34,1]{2,1,0:T(8,128)(2,1)S(1)} %get-tuple-element.75), channel_id=1, source_target_pairs={{0,1},{1,2},{2,3},{4,5},{5,6},{6,7},{8,9},{9,10},{10,11},{12,13},{... | collective-permute-start | bytes 620 | tf_op jit(solution)/shard_map/ppermute | solution.py:19
  12.6 6.7 %collective-permute-start.7 = (bf16[3,34,1]{2,1,0:T(8,128)(2,1)S(1)}, bf16[3,34,1]{2,1,0:T(8,128)(2,1)S(1)}, u32[]{:S(2)}, u32[]{:S(2)}) collective-permute-start(bf16[3,34,1]{2,1,0:T(8,128)(2,1)S(1)} %get-tuple-element.76), channel_id=1, source_target_pairs={{1,0},{2,1},{3,2},{5,4},{6,5},{7,6},{9,8},{10,9},{11,10},{13,12},{... | collective-permute-start | bytes 620 | tf_op jit(solution)/shard_map/ppermute | solution.py:21
  13.9 5.8 %collective-permute-start = (bf16[128,1,128]{0,1,2:T(2,128)(2,1)S(1)}, bf16[128,1,128]{0,1,2:T(2,128)(2,1)}, u32[]{:S(2)}, u32[]{:S(2)}) collective-permute-start(bf16[128,1,128]{0,1,2:T(2,128)(2,1)S(1)} %get-tuple-element.47), channel_id=1, source_target_pairs={{0,4},{4,8},{8,12},{1,5},{5,9},{9,13},{2,6},{6,10},{10,14},{3,7},{... | collective-permute-start | bytes 98312 | tf_op jit(solution)/shard_map/ppermute | solution.py:19
  18.0 6.3 %collective-permute-start.1 = (bf16[128,1,128]{0,1,2:T(2,128)(2,1)S(1)}, bf16[128,1,128]{0,1,2:T(2,128)(2,1)}, u32[]{:S(2)}, u32[]{:S(2)}) collective-permute-start(bf16[128,1,128]{0,1,2:T(2,128)(2,1)S(1)} %get-tuple-element.48), channel_id=1, source_target_pairs={{4,0},{8,4},{12,8},{5,1},{9,5},{13,9},{6,2},{10,6},{14,10},{7,3},{... | collective-permute-start | bytes 98312 | tf_op jit(solution)/shard_map/ppermute | solution.py:21
  25.8 9.3 %copy-start.1 = (bf16[128,32,128]{2,1,0:T(8,128)(2,1)S(1)}, bf16[128,32,128]{2,1,0:T(8,128)(2,1)}, u32[]{:S(2)}) copy-start(bf16[128,32,128]{2,1,0:T(8,128)(2,1)} %param.5) | copy-start | bytes 3145732
  26.8 11.0 %collective-permute-start.2 = (bf16[128,34,1]{0,1,2:T(8,128)(2,1)}, bf16[128,34,1]{0,1,2:T(8,128)(2,1)}, u32[]{:S(2)}, u32[]{:S(2)}) collective-permute-start(bf16[128,34,1]{0,1,2:T(8,128)(2,1)} %get-tuple-element.37), channel_id=1, source_target_pairs={{0,1},{1,2},{2,3},{4,5},{5,6},{6,7},{8,9},{9,10},{10,11},{12,13},{... | collective-permute-start | bytes 26120 | tf_op jit(solution)/shard_map/ppermute | solution.py:19
  30.7 9.2 %collective-permute-start.3 = (bf16[128,34,1]{0,1,2:T(8,128)(2,1)}, bf16[128,34,1]{0,1,2:T(8,128)(2,1)}, u32[]{:S(2)}, u32[]{:S(2)}) collective-permute-start(bf16[128,34,1]{0,1,2:T(8,128)(2,1)} %get-tuple-element.38), channel_id=1, source_target_pairs={{1,0},{2,1},{3,2},{5,4},{6,5},{7,6},{9,8},{10,9},{11,10},{13,12},{... | collective-permute-start | bytes 26120 | tf_op jit(solution)/shard_map/ppermute | solution.py:21
  35.2 2.1 %copy-start.4 = (bf16[3,3,64,128]{3,2,1,0:T(8,128)(2,1)S(1)}, bf16[3,3,64,128]{3,2,1,0:T(8,128)(2,1)}, u32[]{:S(2)}) copy-start(bf16[3,3,64,128]{3,2,1,0:T(8,128)(2,1)} %param.7) | copy-start | bytes 442372
  44.3 1.6 copy-start.3
  58.5 18.8 %copy-start.5 = (s32[8,512]{1,0:T(8,128)S(1)}, s32[8,512]{1,0:T(8,128)}, u32[]{:S(2)}) copy-start(s32[8,512]{1,0:T(8,128)} %param.9) | copy-start | bytes 49156
  58.6 7.6 %collective-permute-start.10 = (f32[1,1,512]{2,1,0:T(1,128)S(1)}, f32[1,1,512]{2,1,0:T(1,128)S(1)}, u32[]{:S(2)}, u32[]{:S(2)}) collective-permute-start(f32[1,1,512]{2,1,0:T(1,128)S(1)} %get-tuple-element.89), channel_id=1, source_target_pairs={{0,1},{1,2},{2,3},{3,4},{4,5},{5,6},{6,7},{7,8},{8,9},{9,10},{10,1... | collective-permute-start | bytes 6152 | tf_op jit(solution)/shard_map/ppermute | solution.py:19
  60.0 6.2 %collective-permute-start.11 = (f32[1,1,512]{2,1,0:T(1,128)S(1)}, f32[1,1,512]{2,1,0:T(1,128)S(1)}, u32[]{:S(2)}, u32[]{:S(2)}) collective-permute-start(f32[1,1,512]{2,1,0:T(1,128)S(1)} %get-tuple-element.90), channel_id=1, source_target_pairs={{1,0},{2,1},{3,2},{4,3},{5,4},{6,5},{7,6},{8,7},{9,8},{10,9},{11,1... | collective-permute-start | bytes 6152 | tf_op jit(solution)/shard_map/ppermute | solution.py:21
  61.3 5.1 %collective-permute-start.8 = (f32[3,1,512]{2,1,0:T(1,128)S(1)}, f32[3,1,512]{2,1,0:T(1,128)S(1)}, u32[]{:S(2)}, u32[]{:S(2)}) collective-permute-start(f32[3,1,512]{2,1,0:T(1,128)S(1)} %get-tuple-element.71), channel_id=1, source_target_pairs={{0,1},{1,2},{2,3},{3,4},{4,5},{5,6},{6,7},{7,8},{8,9},{9,10},{10,1... | collective-permute-start | bytes 18440 | tf_op jit(solution)/shard_map/ppermute | solution.py:19
  64.8 4.3 %collective-permute-start.9 = (f32[3,1,512]{2,1,0:T(1,128)S(1)}, f32[3,1,512]{2,1,0:T(1,128)S(1)}, u32[]{:S(2)}, u32[]{:S(2)}) collective-permute-start(f32[3,1,512]{2,1,0:T(1,128)S(1)} %get-tuple-element.72), channel_id=1, source_target_pairs={{1,0},{2,1},{3,2},{4,3},{5,4},{6,5},{7,6},{8,7},{9,8},{10,9},{11,1... | collective-permute-start | bytes 18440 | tf_op jit(solution)/shard_map/ppermute | solution.py:21
  69.5 5.6 %collective-permute-start.12 = (f32[4,1,512]{2,1,0:T(1,128)S(1)}, f32[4,1,512]{2,1,0:T(1,128)S(1)}, u32[]{:S(2)}, u32[]{:S(2)}) collective-permute-start(f32[4,1,512]{2,1,0:T(1,128)S(1)} %get-tuple-element.69), channel_id=1, source_target_pairs={{0,1},{1,2},{2,3},{3,4},{4,5},{5,6},{6,7},{7,8},{8,9},{9,10},{10,1... | collective-permute-start | bytes 24584 | tf_op jit(solution)/shard_map/ppermute | solution.py:19
  73.8 3.3 %collective-permute-start.13 = (f32[4,1,512]{2,1,0:T(1,128)S(1)}, f32[4,1,512]{2,1,0:T(1,128)S(1)}, u32[]{:S(2)}, u32[]{:S(2)}) collective-permute-start(f32[4,1,512]{2,1,0:T(1,128)S(1)} %get-tuple-element.70), channel_id=1, source_target_pairs={{1,0},{2,1},{3,2},{4,3},{5,4},{6,5},{7,6},{8,7},{9,8},{10,9},{11,1... | collective-permute-start | bytes 24584 | tf_op jit(solution)/shard_map/ppermute | solution.py:21
  77.4 7.2 %collective-permute-start.14 = (f32[1,1,512]{2,1,0:T(1,128)S(1)}, f32[1,1,512]{2,1,0:T(1,128)S(1)}, u32[]{:S(2)}, u32[]{:S(2)}) collective-permute-start(f32[1,1,512]{2,1,0:T(1,128)S(1)} %get-tuple-element.87), channel_id=1, source_target_pairs={{0,1},{1,2},{2,3},{3,4},{4,5},{5,6},{6,7},{7,8},{8,9},{9,10},{10,1... | collective-permute-start | bytes 6152 | tf_op jit(solution)/shard_map/ppermute | solution.py:19
  83.3 3.1 %collective-permute-start.15 = (f32[1,1,512]{2,1,0:T(1,128)S(1)}, f32[1,1,512]{2,1,0:T(1,128)S(1)}, u32[]{:S(2)}, u32[]{:S(2)}) collective-permute-start(f32[1,1,512]{2,1,0:T(1,128)S(1)} %get-tuple-element.88), channel_id=1, source_target_pairs={{1,0},{2,1},{3,2},{4,3},{5,4},{6,5},{7,6},{8,7},{9,8},{10,9},{11,1... | collective-permute-start | bytes 6152 | tf_op jit(solution)/shard_map/ppermute | solution.py:21
  86.9 6.0 %collective-permute-start.16 = (f32[4,1,512]{2,1,0:T(1,128)S(1)}, f32[4,1,512]{2,1,0:T(1,128)S(1)}, u32[]{:S(2)}, u32[]{:S(2)}) collective-permute-start(f32[4,1,512]{2,1,0:T(1,128)S(1)} %get-tuple-element.67), channel_id=1, source_target_pairs={{0,1},{1,2},{2,3},{3,4},{4,5},{5,6},{6,7},{7,8},{8,9},{9,10},{10,1... | collective-permute-start | bytes 24584 | tf_op jit(solution)/shard_map/ppermute | solution.py:19
  91.6 3.1 %collective-permute-start.17 = (f32[4,1,512]{2,1,0:T(1,128)S(1)}, f32[4,1,512]{2,1,0:T(1,128)S(1)}, u32[]{:S(2)}, u32[]{:S(2)}) collective-permute-start(f32[4,1,512]{2,1,0:T(1,128)S(1)} %get-tuple-element.68), channel_id=1, source_target_pairs={{1,0},{2,1},{3,2},{4,3},{5,4},{6,5},{7,6},{8,7},{9,8},{10,9},{11,1... | collective-permute-start | bytes 24584 | tf_op jit(solution)/shard_map/ppermute | solution.py:21
  129.9 2.6 %collective-permute-start.18 = (f32[1,1,512]{2,1,0:T(1,128)S(1)}, f32[1,1,512]{2,1,0:T(1,128)S(1)}, u32[]{:S(2)}, u32[]{:S(2)}) collective-permute-start(f32[1,1,512]{2,1,0:T(1,128)S(1)} %get-tuple-element.85), channel_id=1, source_target_pairs={{0,1},{1,2},{2,3},{3,4},{4,5},{5,6},{6,7},{7,8},{8,9},{9,10},{10,1... | collective-permute-start | bytes 6152 | tf_op jit(solution)/shard_map/ppermute | solution.py:19
  131.2 3.1 %collective-permute-start.19 = (f32[1,1,512]{2,1,0:T(1,128)S(1)}, f32[1,1,512]{2,1,0:T(1,128)S(1)}, u32[]{:S(2)}, u32[]{:S(2)}) collective-permute-start(f32[1,1,512]{2,1,0:T(1,128)S(1)} %get-tuple-element.86), channel_id=1, source_target_pairs={{1,0},{2,1},{3,2},{4,3},{5,4},{6,5},{7,6},{8,7},{9,8},{10,9},{11,1... | collective-permute-start | bytes 6152 | tf_op jit(solution)/shard_map/ppermute | solution.py:21
  134.8 3.4 %collective-permute-start.20 = (f32[4,1,512]{2,1,0:T(1,128)S(1)}, f32[4,1,512]{2,1,0:T(1,128)S(1)}, u32[]{:S(2)}, u32[]{:S(2)}) collective-permute-start(f32[4,1,512]{2,1,0:T(1,128)S(1)} %get-tuple-element.65), channel_id=1, source_target_pairs={{0,1},{1,2},{2,3},{3,4},{4,5},{5,6},{6,7},{7,8},{8,9},{9,10},{10,1... | collective-permute-start | bytes 24584 | tf_op jit(solution)/shard_map/ppermute | solution.py:19
  136.9 3.1 %collective-permute-start.21 = (f32[4,1,512]{2,1,0:T(1,128)S(1)}, f32[4,1,512]{2,1,0:T(1,128)S(1)}, u32[]{:S(2)}, u32[]{:S(2)}) collective-permute-start(f32[4,1,512]{2,1,0:T(1,128)S(1)} %get-tuple-element.66), channel_id=1, source_target_pairs={{1,0},{2,1},{3,2},{4,3},{5,4},{6,5},{7,6},{8,7},{9,8},{10,9},{11,1... | collective-permute-start | bytes 24584 | tf_op jit(solution)/shard_map/ppermute | solution.py:21
where the time goes:
time: 179 us; the launch traced here: 178 us
  blocking collectives  77 us (43%)
  starting transfers between devices  51.5 us (29%)
  waiting for transfers between devices  17.9 us (10%)
  local copies, waits for them, and re-layouts  10.2 us (6%)
  other arithmetic  9.49 us (5%)
  between operations  6.62 us (4%)
  matrix products  5.29 us (3%)
    psum x2, blocking collectives, global_sums(): return lax.psum((values[0], values[1]), ('rows', 'cols', 'sub'))  65 us
    ppermute x11, starting transfers between devices, with_halo(): lax.ppermute(tail, axis, [(i, (i + 1) % count) for i in range(ends)])  37.3 us
    ppermute x11, waiting for transfers between devices, with_halo(): lax.ppermute(head, axis, [((i + 1) % count, i) for i in range(ends)])  17.8 us
    ppermute x11, starting transfers between devices, with_halo(): lax.ppermute(head, axis, [((i + 1) % count, i) for i in range(ends)])  14.2 us
    all_to_all x1, blocking collectives, on_device(): lax.all_to_all(stacked, ('cols', 'sub'), split_axis=1, concat_axis=2, til...  12 us
    concatenate x7, other arithmetic, with_halo(): jnp.concatenate([lax.ppermute(tail, axis, [(i, (i + 1) % count) for i in...  5.03 us
    dot_general x9, matrix products, head_maps(): jnp.dot(conv_weight[shift_r, shift_c], window_cell_count, preferred_eleme...  4.64 us
  transfers between devices with their start and end apart: 22, of which 8 were waited for; matrix products, arithmetic and copies ran while one was open for 6% of the time, Pallas kernels for 0%

commit v1 on v0

--- a/solution.py
+++ b/solution.py
@@ -6,6 +6,11 @@
 ITERS = 2
 RIDGE = 0.05
 BASE_WEIGHT = 0.1
+
+
+def axis_by_axis(x, inner_axis, outer_axis):
+    half = lax.psum(x, inner_axis)
+    return lax.psum(half, outer_axis)
 
 
 def with_halo(cells, sides, width):
@@ -113,7 +118,7 @@
 
 
 def global_sums(values):
-    return lax.psum((values[0], values[1]), ("rows", "cols", "sub"))
+    return axis_by_axis((values[0], values[1]), ("cols", "sub"), "rows")
 
 
 def on_device(features, guide_image, conv_weight, head_weight, pixel_mask):

time: 179 us -> 159 us (0.89)
  blocking collectives: 77 us -> 54.1 us
  starting transfers between devices: 51.5 us -> 53.7 us
    psum x2 -> x4, blocking collectives: 65 us -> 42.1 us  [the longest x2 22.9 us: axis_by_axis(): half = lax.psum(x, inner_axis)]
    ppermute x11, starting transfers between devices: 37.3 us -> 39.5 us  [with_halo(): lax.ppermute(tail, axis, [(i, (i + 1) % count) for i in range(ends)])]
  transfers between devices with their start and end apart: 22 -> 22, of which waited for: 8 -> 8; matrix products, arithmetic and copies ran while one was open for 6% -> 7% of each run, Pallas kernels for 0% -> 0%
where the time goes in v1:
time: 159 us; the launch traced here: 158 us
  blocking collectives  54.1 us (34%)
  starting transfers between devices  53.7 us (34%)
  waiting for transfers between devices  18.5 us (12%)
  local copies, waits for them, and re-layouts  10.2 us (6%)
  other arithmetic  9.55 us (6%)
  between operations  6.78 us (4%)
  matrix products  5.29 us (3%)
    ppermute x11, starting transfers between devices, with_halo(): lax.ppermute(tail, axis, [(i, (i + 1) % count) for i in range(ends)])  39.5 us
    psum x2, blocking collectives, axis_by_axis(): half = lax.psum(x, inner_axis)  22.9 us
    psum x2, blocking collectives, axis_by_axis(): return lax.psum(half, outer_axis)  19.2 us
    ppermute x11, waiting for transfers between devices, with_halo(): lax.ppermute(head, axis, [((i + 1) % count, i) for i in range(ends)])  18.5 us
    ppermute x11, starting transfers between devices, with_halo(): lax.ppermute(head, axis, [((i + 1) % count, i) for i in range(ends)])  14.2 us
    all_to_all x1, blocking collectives, on_device(): lax.all_to_all(stacked, ('cols', 'sub'), split_axis=1, concat_axis=2, til...  11.9 us
    concatenate x7, other arithmetic, with_halo(): jnp.concatenate([lax.ppermute(tail, axis, [(i, (i + 1) % count) for i in...  5.03 us
    dot_general x9, matrix products, head_maps(): jnp.dot(conv_weight[shift_r, shift_c], window_cell_count, preferred_eleme...  4.64 us
  transfers between devices with their start and end apart: 22, of which 8 were waited for; matrix products, arithmetic and copies ran while one was open for 7% of the time, Pallas kernels for 0%

profile of v1, /device:TPU:0, one launch (start us, length us, event | category | flops | bytes accessed | tf_op | source)
XLA Modules:
  0.0 158.2 jit_solution(14834688065611317212)
XLA Ops:
  0.0 0.8 fusion.96
  0.8 4.9 %collective-permute-start.4 = (bf16[3,1,128]{2,1,0:T(2,128)(2,1)S(1)}, bf16[3,1,128]{2,1,0:T(2,128)(2,1)S(1)}, u32[]{:S(2)}, u32[]{:S(2)}) collective-permute-start(bf16[3,1,128]{2,1,0:T(2,128)(2,1)S(1)} %get-tuple-element.81), channel_id=1, source_target_pairs={{0,4},{4,8},{8,12},{1,5},{5,9},{9,13},{2,6},{6,10},{10,14},{3,7},{... | collective-permute-start | bytes 2312 | tf_op jit(solution)/shard_map/ppermute | solution.py:24
  5.7 1.3 collective-permute-start.5
  7.0 2.5 %copy.68 = bf16[128,32,128]{0,1,2:T(8,128)(2,1)S(1)} copy(bf16[128,32,128]{2,1,0:T(8,128)(2,1)} %param.5) | data formatting | bytes 2097152 | tf_op args[0]
  9.6 1.6 collective-permute-done.5
  11.3 1.3 collective-permute-start.6
  12.6 1.3 collective-permute-start.7
  13.9 4.1 %collective-permute-start = (bf16[128,1,128]{0,1,2:T(2,128)(2,1)S(1)}, bf16[128,1,128]{0,1,2:T(2,128)(2,1)}, u32[]{:S(2)}, u32[]{:S(2)}) collective-permute-start(bf16[128,1,128]{0,1,2:T(2,128)(2,1)S(1)} %get-tuple-element.51), channel_id=1, source_target_pairs={{0,4},{4,8},{8,12},{1,5},{5,9},{9,13},{2,6},{6,10},{10,14},{3,7},{... | collective-permute-start | bytes 98312 | tf_op jit(solution)/shard_map/ppermute | solution.py:24
  18.0 1.3 collective-permute-start.1
  19.7 4.5 %collective-permute-done.1 = bf16[128,1,128]{0,1,2:T(2,128)(2,1)} collective-permute-done((bf16[128,1,128]{0,1,2:T(2,128)(2,1)S(1)}, bf16[128,1,128]{0,1,2:T(2,128)(2,1)}, u32[]{:S(2)}, u32[]{:S(2)}) %collective-permute-start.1) | collective-permute-done | bytes 32800 | tf_op jit(solution)/shard_map/ppermute | solution.py:26
  24.2 1.6 %pad_maximum_fusion = bf16[128,34,128]{0,1,2:T(8,128)(2,1)S(1)} fusion(bf16[128,1,128]{0,1,2:T(2,128)(2,1)} %collective-permute-done.1, bf16[128,32,128]{0,1,2:T(8,128)(2,1)S(1)} %copy.68, bf16[128,1,128]{0,1,2:T(2,128)(2,1)} %collective-permute-done), kind=kLoop, calls=%fused_computation.17 | loop fusion | flops 3342336 | bytes 2228224 | tf_op jit(solution)/shard_map/concatenate | solution.py:22
  26.8 3.9 %collective-permute-start.2 = (bf16[128,34,1]{0,1,2:T(8,128)(2,1)}, bf16[128,34,1]{0,1,2:T(8,128)(2,1)}, u32[]{:S(2)}, u32[]{:S(2)}) collective-permute-start(bf16[128,34,1]{0,1,2:T(8,128)(2,1)} %get-tuple-element.41), channel_id=1, source_target_pairs={{0,1},{1,2},{2,3},{4,5},{5,6},{6,7},{8,9},{9,10},{10,11},{12,13},{... | collective-permute-start | bytes 26120 | tf_op jit(solution)/shard_map/ppermute | solution.py:24
  30.7 1.3 collective-permute-start.3
  32.0 1.6 %copy.73 = bf16[128,1,128]{2,1,0:T(2,128)(2,1)} copy(bf16[128,1,128]{0,1,2:T(2,128)(2,1)} %collective-permute-done) | data formatting | bytes 65536 | tf_op jit(solution)/shard_map/ppermute | solution.py:24
  33.6 1.6 %copy.76 = bf16[128,1,128]{2,1,0:T(2,128)(2,1)} copy(bf16[128,1,128]{0,1,2:T(2,128)(2,1)} %collective-permute-done.1) | data formatting | bytes 65536 | tf_op jit(solution)/shard_map/ppermute | solution.py:26
  35.2 2.1 %pad_maximum_fusion.3 = (bf16[128,32,128]{2,1,0:T(8,128)(2,1)S(1)}, bf16[128,32,128]{2,1,0:T(8,128)(2,1)S(1)}) fusion(bf16[128,32,128]{2,1,0:T(8,128)(2,1)S(1)} %copy-done.1, bf16[128,1,128]{2,1,0:T(2,128)(2,1)} %copy.73, bf16[128,1,128]{2,1,0:T(2,128)(2,1)} %copy.76), kind=kLoop, calls=%fused_computation.30 | loop fusion | flops 4194304 | bytes 3211264 | tf_op jit(solution)/shard_map/concatenate | solution.py:22
  37.8 0.7 copy.71
  38.5 0.8 fusion.6
  39.9 0.7 constant_dynamic-update-slice_fusion
  40.6 0.8 fusion.90
  44.3 0.8 fusion.4
  46.3 11.9 %all_to_all.15 = f32[14,32,128]{2,0,1:T(8,128)S(1)} all-to-all(f32[14,32,128]{2,0,1:T(8,128)S(1)} %copy.77), channel_id=1, replica_groups=mesh['groups'=2,'rows'=4,'cols'=2,'sub'=2] {'cols','sub'}, dimensions={1} | all-to-all | bytes 458752 | tf_op jit(solution)/shard_map/all_to_all | solution.py:135
  58.6 1.4 collective-permute-start.10
  59.9 1.3 collective-permute-start.11
  61.3 3.5 %collective-permute-start.8 = (f32[3,1,512]{2,1,0:T(1,128)S(1)}, f32[3,1,512]{2,1,0:T(1,128)S(1)}, u32[]{:S(2)}, u32[]{:S(2)}) collective-permute-start(f32[3,1,512]{2,1,0:T(1,128)S(1)} %get-tuple-element.75), channel_id=1, source_target_pairs={{0,1},{1,2},{2,3},{3,4},{4,5},{5,6},{6,7},{7,8},{8,9},{9,10},{10,1... | collective-permute-start | bytes 18440 | tf_op jit(solution)/shard_map/ppermute | solution.py:24
  64.8 1.3 collective-permute-start.9
  66.3 2.8 %collective-permute-done.9 = f32[3,1,512]{2,1,0:T(1,128)S(1)} collective-permute-done((f32[3,1,512]{2,1,0:T(1,128)S(1)}, f32[3,1,512]{2,1,0:T(1,128)S(1)}, u32[]{:S(2)}, u32[]{:S(2)}) %collective-permute-start.9) | collective-permute-done | bytes 6176 | tf_op jit(solution)/shard_map/ppermute | solution.py:26
  69.5 4.3 %collective-permute-start.12 = (f32[4,1,512]{2,1,0:T(1,128)S(1)}, f32[4,1,512]{2,1,0:T(1,128)S(1)}, u32[]{:S(2)}, u32[]{:S(2)}) collective-permute-start(f32[4,1,512]{2,1,0:T(1,128)S(1)} %get-tuple-element.73), channel_id=1, source_target_pairs={{0,1},{1,2},{2,3},{3,4},{4,5},{5,6},{6,7},{7,8},{8,9},{9,10},{10,1... | collective-permute-start | bytes 24584 | tf_op jit(solution)/shard_map/ppermute | solution.py:24
  73.8 1.3 collective-permute-start.13
  75.1 2.0 %collective-permute-done.13 = f32[4,1,512]{2,1,0:T(1,128)S(1)} collective-permute-done((f32[4,1,512]{2,1,0:T(1,128)S(1)}, f32[4,1,512]{2,1,0:T(1,128)S(1)}, u32[]{:S(2)}, u32[]{:S(2)}) %collective-permute-start.13) | collective-permute-done | bytes 8224 | tf_op jit(solution)/shard_map/ppermute | solution.py:26
  77.4 5.9 %collective-permute-start.14 = (f32[1,1,512]{2,1,0:T(1,128)S(1)}, f32[1,1,512]{2,1,0:T(1,128)S(1)}, u32[]{:S(2)}, u32[]{:S(2)}) collective-permute-start(f32[1,1,512]{2,1,0:T(1,128)S(1)} %get-tuple-element.91), channel_id=1, source_target_pairs={{0,1},{1,2},{2,3},{3,4},{4,5},{5,6},{6,7},{7,8},{8,9},{9,10},{10,1... | collective-permute-start | bytes 6152 | tf_op jit(solution)/shard_map/ppermute | solution.py:24
  83.3 1.3 collective-permute-start.15
  84.6 1.7 %collective-permute-done.15 = f32[1,1,512]{2,1,0:T(1,128)S(1)} collective-permute-done((f32[1,1,512]{2,1,0:T(1,128)S(1)}, f32[1,1,512]{2,1,0:T(1,128)S(1)}, u32[]{:S(2)}, u32[]{:S(2)}) %collective-permute-start.15) | collective-permute-done | bytes 2080 | tf_op jit(solution)/shard_map/ppermute | solution.py:26
  86.9 4.7 %collective-permute-start.16 = (f32[4,1,512]{2,1,0:T(1,128)S(1)}, f32[4,1,512]{2,1,0:T(1,128)S(1)}, u32[]{:S(2)}, u32[]{:S(2)}) collective-permute-start(f32[4,1,512]{2,1,0:T(1,128)S(1)} %get-tuple-element.71), channel_id=1, source_target_pairs={{0,1},{1,2},{2,3},{3,4},{4,5},{5,6},{6,7},{7,8},{8,9},{9,10},{10,1... | collective-permute-start | bytes 24584 | tf_op jit(solution)/shard_map/ppermute | solution.py:24
  91.6 1.3 collective-permute-start.17
  92.9 1.8 %collective-permute-done.17 = f32[4,1,512]{2,1,0:T(1,128)S(1)} collective-permute-done((f32[4,1,512]{2,1,0:T(1,128)S(1)}, f32[4,1,512]{2,1,0:T(1,128)S(1)}, u32[]{:S(2)}, u32[]{:S(2)}) %collective-permute-start.17) | collective-permute-done | bytes 8224 | tf_op jit(solution)/shard_map/ppermute | solution.py:26
  94.9 0.7 multiply_reduce_fusion.1
  95.6 11.3 %all-reduce.8 = (f32[]{:T(128)}, f32[]{:T(128)}) all-reduce(f32[]{:T(128)} %get-tuple-element.8, f32[]{:T(128)} %get-tuple-element.7), channel_id=1, replica_groups=mesh['groups'=2,'rows'=4,'cols'=2,'sub'=2] {'cols','sub'}, use_global_device_ids=true, to_apply=%region_1.2 | all-reduce | flops 2 | bytes 16 | tf_op jit(solution)/shard_map/psum | solution.py:12
  106.9 10.1 %all-reduce.10 = (f32[]{:T(128)}, f32[]{:T(128)}) all-reduce(f32[]{:T(128)} %get-tuple-element.11, f32[]{:T(128)} %get-tuple-element.12), channel_id=1, replica_groups=mesh['groups'=2,'rows'=4,'cols'=2,'sub'=2] {'rows'}, use_global_device_ids=true, to_apply=%region_2.3 | all-reduce | flops 2 | bytes 16 | tf_op jit(solution)/shard_map/psum | solution.py:13
  118.5 1.3 collective-permute-start.18
  119.8 1.3 collective-permute-start.19
  121.1 2.4 %collective-permute-done.19 = f32[1,1,512]{2,1,0:T(1,128)S(1)} collective-permute-done((f32[1,1,512]{2,1,0:T(1,128)S(1)}, f32[1,1,512]{2,1,0:T(1,128)S(1)}, u32[]{:S(2)}, u32[]{:S(2)}) %collective-permute-start.19) | collective-permute-done | bytes 2080 | tf_op jit(solution)/shard_map/ppermute | solution.py:26
  124.0 4.3 %collective-permute-start.20 = (f32[4,1,512]{2,1,0:T(1,128)S(1)}, f32[4,1,512]{2,1,0:T(1,128)S(1)}, u32[]{:S(2)}, u32[]{:S(2)}) collective-permute-start(f32[4,1,512]{2,1,0:T(1,128)S(1)} %get-tuple-element.69), channel_id=1, source_target_pairs={{0,1},{1,2},{2,3},{3,4},{4,5},{5,6},{6,7},{7,8},{8,9},{9,10},{10,1... | collective-permute-start | bytes 24584 | tf_op jit(solution)/shard_map/ppermute | solution.py:24
  128.3 1.3 collective-permute-start.21
  129.6 1.8 %collective-permute-done.21 = f32[4,1,512]{2,1,0:T(1,128)S(1)} collective-permute-done((f32[4,1,512]{2,1,0:T(1,128)S(1)}, f32[4,1,512]{2,1,0:T(1,128)S(1)}, u32[]{:S(2)}, u32[]{:S(2)}) %collective-permute-start.21) | collective-permute-done | bytes 8224 | tf_op jit(solution)/shard_map/ppermute | solution.py:26
  131.6 0.7 fusion.29
  132.3 11.6 %all-reduce.7 = (f32[]{:T(128)}, f32[]{:T(128)}) all-reduce(f32[]{:T(128)} %get-tuple-element.6, f32[]{:T(128)} %get-tuple-element.5), channel_id=1, replica_groups=mesh['groups'=2,'rows'=4,'cols'=2,'sub'=2] {'cols','sub'}, use_global_device_ids=true, to_apply=%region_7.8 | all-reduce | flops 2 | bytes 16 | tf_op jit(solution)/shard_map/psum | solution.py:12
  143.9 9.1 %all-reduce.9 = (f32[]{:T(128)}, f32[]{:T(128)}) all-reduce(f32[]{:T(128)} %get-tuple-element.9, f32[]{:T(128)} %get-tuple-element.10), channel_id=1, replica_groups=mesh['groups'=2,'rows'=4,'cols'=2,'sub'=2] {'rows'}, use_global_device_ids=true, to_apply=%region_8.9 | all-reduce | flops 2 | bytes 16 | tf_op jit(solution)/shard_map/psum | solution.py:13
  (107 shorter events, 9.7 us)
Async XLA Ops:
  0.0 45.1 %copy-start = (f32[2,64]{1,0:T(2,128)S(1)}, f32[2,64]{1,0:T(2,128)}, u32[]{:S(2)}) copy-start(f32[2,64]{1,0:T(2,128)} %param.8) | copy-start | bytes 1540
  0.0 11.2 %copy-start.2 = (bf16[3,32,128]{2,1,0:T(8,128)(2,1)S(1)}, bf16[3,32,128]{2,1,0:T(8,128)(2,1)}, u32[]{:S(2)}) copy-start(bf16[3,32,128]{2,1,0:T(8,128)(2,1)} %param.6) | copy-start | bytes 73732
  0.8 8.8 %collective-permute-start.4 = (bf16[3,1,128]{2,1,0:T(2,128)(2,1)S(1)}, bf16[3,1,128]{2,1,0:T(2,128)(2,1)S(1)}, u32[]{:S(2)}, u32[]{:S(2)}) collective-permute-start(bf16[3,1,128]{2,1,0:T(2,128)(2,1)S(1)} %get-tuple-element.81), channel_id=1, source_target_pairs={{0,4},{4,8},{8,12},{1,5},{5,9},{9,13},{2,6},{6,10},{10,14},{3,7},{... | collective-permute-start | bytes 2312 | tf_op jit(solution)/shard_map/ppermute | solution.py:24
  5.7 5.5 %collective-permute-start.5 = (bf16[3,1,128]{2,1,0:T(2,128)(2,1)S(1)}, bf16[3,1,128]{2,1,0:T(2,128)(2,1)S(1)}, u32[]{:S(2)}, u32[]{:S(2)}) collective-permute-start(bf16[3,1,128]{2,1,0:T(2,128)(2,1)S(1)} %get-tuple-element.82), channel_id=1, source_target_pairs={{4,0},{8,4},{12,8},{5,1},{9,5},{13,9},{6,2},{10,6},{14,10},{7,3},{... | collective-permute-start | bytes 2312 | tf_op jit(solution)/shard_map/ppermute | solution.py:26
  11.3 8.0 %collective-permute-start.6 = (bf16[3,34,1]{2,1,0:T(8,128)(2,1)S(1)}, bf16[3,34,1]{2,1,0:T(8,128)(2,1)S(1)}, u32[]{:S(2)}, u32[]{:S(2)}) collective-permute-start(bf16[3,34,1]{2,1,0:T(8,128)(2,1)S(1)} %get-tuple-element.79), channel_id=1, source_target_pairs={{0,1},{1,2},{2,3},{4,5},{5,6},{6,7},{8,9},{9,10},{10,11},{12,13},{... | collective-permute-start | bytes 620 | tf_op jit(solution)/shard_map/ppermute | solution.py:24
  12.6 6.7 %collective-permute-start.7 = (bf16[3,34,1]{2,1,0:T(8,128)(2,1)S(1)}, bf16[3,34,1]{2,1,0:T(8,128)(2,1)S(1)}, u32[]{:S(2)}, u32[]{:S(2)}) collective-permute-start(bf16[3,34,1]{2,1,0:T(8,128)(2,1)S(1)} %get-tuple-element.80), channel_id=1, source_target_pairs={{1,0},{2,1},{3,2},{5,4},{6,5},{7,6},{9,8},{10,9},{11,10},{13,12},{... | collective-permute-start | bytes 620 | tf_op jit(solution)/shard_map/ppermute | solution.py:26
  13.9 5.8 %collective-permute-start = (bf16[128,1,128]{0,1,2:T(2,128)(2,1)S(1)}, bf16[128,1,128]{0,1,2:T(2,128)(2,1)}, u32[]{:S(2)}, u32[]{:S(2)}) collective-permute-start(bf16[128,1,128]{0,1,2:T(2,128)(2,1)S(1)} %get-tuple-element.51), channel_id=1, source_target_pairs={{0,4},{4,8},{8,12},{1,5},{5,9},{9,13},{2,6},{6,10},{10,14},{3,7},{... | collective-permute-start | bytes 98312 | tf_op jit(solution)/shard_map/ppermute | solution.py:24
  18.0 6.3 %collective-permute-start.1 = (bf16[128,1,128]{0,1,2:T(2,128)(2,1)S(1)}, bf16[128,1,128]{0,1,2:T(2,128)(2,1)}, u32[]{:S(2)}, u32[]{:S(2)}) collective-permute-start(bf16[128,1,128]{0,1,2:T(2,128)(2,1)S(1)} %get-tuple-element.52), channel_id=1, source_target_pairs={{4,0},{8,4},{12,8},{5,1},{9,5},{13,9},{6,2},{10,6},{14,10},{7,3},{... | collective-permute-start | bytes 98312 | tf_op jit(solution)/shard_map/ppermute | solution.py:26
  25.8 9.3 %copy-start.1 = (bf16[128,32,128]{2,1,0:T(8,128)(2,1)S(1)}, bf16[128,32,128]{2,1,0:T(8,128)(2,1)}, u32[]{:S(2)}) copy-start(bf16[128,32,128]{2,1,0:T(8,128)(2,1)} %param.5) | copy-start | bytes 3145732
  26.8 11.0 %collective-permute-start.2 = (bf16[128,34,1]{0,1,2:T(8,128)(2,1)}, bf16[128,34,1]{0,1,2:T(8,128)(2,1)}, u32[]{:S(2)}, u32[]{:S(2)}) collective-permute-start(bf16[128,34,1]{0,1,2:T(8,128)(2,1)} %get-tuple-element.41), channel_id=1, source_target_pairs={{0,1},{1,2},{2,3},{4,5},{5,6},{6,7},{8,9},{9,10},{10,11},{12,13},{... | collective-permute-start | bytes 26120 | tf_op jit(solution)/shard_map/ppermute | solution.py:24
  30.7 9.2 %collective-permute-start.3 = (bf16[128,34,1]{0,1,2:T(8,128)(2,1)}, bf16[128,34,1]{0,1,2:T(8,128)(2,1)}, u32[]{:S(2)}, u32[]{:S(2)}) collective-permute-start(bf16[128,34,1]{0,1,2:T(8,128)(2,1)} %get-tuple-element.42), channel_id=1, source_target_pairs={{1,0},{2,1},{3,2},{5,4},{6,5},{7,6},{9,8},{10,9},{11,10},{13,12},{... | collective-permute-start | bytes 26120 | tf_op jit(solution)/shard_map/ppermute | solution.py:26
  35.2 2.1 %copy-start.4 = (bf16[3,3,64,128]{3,2,1,0:T(8,128)(2,1)S(1)}, bf16[3,3,64,128]{3,2,1,0:T(8,128)(2,1)}, u32[]{:S(2)}) copy-start(bf16[3,3,64,128]{3,2,1,0:T(8,128)(2,1)} %param.7) | copy-start | bytes 442372
  44.3 1.6 %copy-start.3 = (bf16[3,32,128]{2,1,0:T(8,128)(2,1)S(1)}, bf16[3,32,128]{2,1,0:T(8,128)(2,1)}, u32[]{:S(2)}) copy-start(bf16[3,32,128]{2,1,0:T(8,128)(2,1)} %param.6) | copy-start | bytes 73732
  58.5 18.9 %copy-start.5 = (s32[8,512]{1,0:T(8,128)S(1)}, s32[8,512]{1,0:T(8,128)}, u32[]{:S(2)}) copy-start(s32[8,512]{1,0:T(8,128)} %param.9) | copy-start | bytes 49156
  58.6 7.6 %collective-permute-start.10 = (f32[1,1,512]{2,1,0:T(1,128)S(1)}, f32[1,1,512]{2,1,0:T(1,128)S(1)}, u32[]{:S(2)}, u32[]{:S(2)}) collective-permute-start(f32[1,1,512]{2,1,0:T(1,128)S(1)} %get-tuple-element.93), channel_id=1, source_target_pairs={{0,1},{1,2},{2,3},{3,4},{4,5},{5,6},{6,7},{7,8},{8,9},{9,10},{10,1... | collective-permute-start | bytes 6152 | tf_op jit(solution)/shard_map/ppermute | solution.py:24
  59.9 6.2 %collective-permute-start.11 = (f32[1,1,512]{2,1,0:T(1,128)S(1)}, f32[1,1,512]{2,1,0:T(1,128)S(1)}, u32[]{:S(2)}, u32[]{:S(2)}) collective-permute-start(f32[1,1,512]{2,1,0:T(1,128)S(1)} %get-tuple-element.94), channel_id=1, source_target_pairs={{1,0},{2,1},{3,2},{4,3},{5,4},{6,5},{7,6},{8,7},{9,8},{10,9},{11,1... | collective-permute-start | bytes 6152 | tf_op jit(solution)/shard_map/ppermute | solution.py:26
  61.3 5.1 %collective-permute-start.8 = (f32[3,1,512]{2,1,0:T(1,128)S(1)}, f32[3,1,512]{2,1,0:T(1,128)S(1)}, u32[]{:S(2)}, u32[]{:S(2)}) collective-permute-start(f32[3,1,512]{2,1,0:T(1,128)S(1)} %get-tuple-element.75), channel_id=1, source_target_pairs={{0,1},{1,2},{2,3},{3,4},{4,5},{5,6},{6,7},{7,8},{8,9},{9,10},{10,1... | collective-permute-start | bytes 18440 | tf_op jit(solution)/shard_map/ppermute | solution.py:24
  64.8 4.3 %collective-permute-start.9 = (f32[3,1,512]{2,1,0:T(1,128)S(1)}, f32[3,1,512]{2,1,0:T(1,128)S(1)}, u32[]{:S(2)}, u32[]{:S(2)}) collective-permute-start(f32[3,1,512]{2,1,0:T(1,128)S(1)} %get-tuple-element.76), channel_id=1, source_target_pairs={{1,0},{2,1},{3,2},{4,3},{5,4},{6,5},{7,6},{8,7},{9,8},{10,9},{11,1... | collective-permute-start | bytes 18440 | tf_op jit(solution)/shard_map/ppermute | solution.py:26
  69.5 5.6 %collective-permute-start.12 = (f32[4,1,512]{2,1,0:T(1,128)S(1)}, f32[4,1,512]{2,1,0:T(1,128)S(1)}, u32[]{:S(2)}, u32[]{:S(2)}) collective-permute-start(f32[4,1,512]{2,1,0:T(1,128)S(1)} %get-tuple-element.73), channel_id=1, source_target_pairs={{0,1},{1,2},{2,3},{3,4},{4,5},{5,6},{6,7},{7,8},{8,9},{9,10},{10,1... | collective-permute-start | bytes 24584 | tf_op jit(solution)/shard_map/ppermute | solution.py:24
  73.8 3.3 %collective-permute-start.13 = (f32[4,1,512]{2,1,0:T(1,128)S(1)}, f32[4,1,512]{2,1,0:T(1,128)S(1)}, u32[]{:S(2)}, u32[]{:S(2)}) collective-permute-start(f32[4,1,512]{2,1,0:T(1,128)S(1)} %get-tuple-element.74), channel_id=1, source_target_pairs={{1,0},{2,1},{3,2},{4,3},{5,4},{6,5},{7,6},{8,7},{9,8},{10,9},{11,1... | collective-permute-start | bytes 24584 | tf_op jit(solution)/shard_map/ppermute | solution.py:26
  77.4 7.2 %collective-permute-start.14 = (f32[1,1,512]{2,1,0:T(1,128)S(1)}, f32[1,1,512]{2,1,0:T(1,128)S(1)}, u32[]{:S(2)}, u32[]{:S(2)}) collective-permute-start(f32[1,1,512]{2,1,0:T(1,128)S(1)} %get-tuple-element.91), channel_id=1, source_target_pairs={{0,1},{1,2},{2,3},{3,4},{4,5},{5,6},{6,7},{7,8},{8,9},{9,10},{10,1... | collective-permute-start | bytes 6152 | tf_op jit(solution)/shard_map/ppermute | solution.py:24
  83.3 3.1 %collective-permute-start.15 = (f32[1,1,512]{2,1,0:T(1,128)S(1)}, f32[1,1,512]{2,1,0:T(1,128)S(1)}, u32[]{:S(2)}, u32[]{:S(2)}) collective-permute-start(f32[1,1,512]{2,1,0:T(1,128)S(1)} %get-tuple-element.92), channel_id=1, source_target_pairs={{1,0},{2,1},{3,2},{4,3},{5,4},{6,5},{7,6},{8,7},{9,8},{10,9},{11,1... | collective-permute-start | bytes 6152 | tf_op jit(solution)/shard_map/ppermute | solution.py:26
  86.9 6.0 %collective-permute-start.16 = (f32[4,1,512]{2,1,0:T(1,128)S(1)}, f32[4,1,512]{2,1,0:T(1,128)S(1)}, u32[]{:S(2)}, u32[]{:S(2)}) collective-permute-start(f32[4,1,512]{2,1,0:T(1,128)S(1)} %get-tuple-element.71), channel_id=1, source_target_pairs={{0,1},{1,2},{2,3},{3,4},{4,5},{5,6},{6,7},{7,8},{8,9},{9,10},{10,1... | collective-permute-start | bytes 24584 | tf_op jit(solution)/shard_map/ppermute | solution.py:24
  91.6 3.1 %collective-permute-start.17 = (f32[4,1,512]{2,1,0:T(1,128)S(1)}, f32[4,1,512]{2,1,0:T(1,128)S(1)}, u32[]{:S(2)}, u32[]{:S(2)}) collective-permute-start(f32[4,1,512]{2,1,0:T(1,128)S(1)} %get-tuple-element.72), channel_id=1, source_target_pairs={{1,0},{2,1},{3,2},{4,3},{5,4},{6,5},{7,6},{8,7},{9,8},{10,9},{11,1... | collective-permute-start | bytes 24584 | tf_op jit(solution)/shard_map/ppermute | solution.py:26
  118.5 2.6 %collective-permute-start.18 = (f32[1,1,512]{2,1,0:T(1,128)S(1)}, f32[1,1,512]{2,1,0:T(1,128)S(1)}, u32[]{:S(2)}, u32[]{:S(2)}) collective-permute-start(f32[1,1,512]{2,1,0:T(1,128)S(1)} %get-tuple-element.89), channel_id=1, source_target_pairs={{0,1},{1,2},{2,3},{3,4},{4,5},{5,6},{6,7},{7,8},{8,9},{9,10},{10,1... | collective-permute-start | bytes 6152 | tf_op jit(solution)/shard_map/ppermute | solution.py:24
  119.8 3.7 %collective-permute-start.19 = (f32[1,1,512]{2,1,0:T(1,128)S(1)}, f32[1,1,512]{2,1,0:T(1,128)S(1)}, u32[]{:S(2)}, u32[]{:S(2)}) collective-permute-start(f32[1,1,512]{2,1,0:T(1,128)S(1)} %get-tuple-element.90), channel_id=1, source_target_pairs={{1,0},{2,1},{3,2},{4,3},{5,4},{6,5},{7,6},{8,7},{9,8},{10,9},{11,1... | collective-permute-start | bytes 6152 | tf_op jit(solution)/shard_map/ppermute | solution.py:26
  124.0 5.6 %collective-permute-start.20 = (f32[4,1,512]{2,1,0:T(1,128)S(1)}, f32[4,1,512]{2,1,0:T(1,128)S(1)}, u32[]{:S(2)}, u32[]{:S(2)}) collective-permute-start(f32[4,1,512]{2,1,0:T(1,128)S(1)} %get-tuple-element.69), channel_id=1, source_target_pairs={{0,1},{1,2},{2,3},{3,4},{4,5},{5,6},{6,7},{7,8},{8,9},{9,10},{10,1... | collective-permute-start | bytes 24584 | tf_op jit(solution)/shard_map/ppermute | solution.py:24
  128.3 3.1 %collective-permute-start.21 = (f32[4,1,512]{2,1,0:T(1,128)S(1)}, f32[4,1,512]{2,1,0:T(1,128)S(1)}, u32[]{:S(2)}, u32[]{:S(2)}) collective-permute-start(f32[4,1,512]{2,1,0:T(1,128)S(1)} %get-tuple-element.70), channel_id=1, source_target_pairs={{1,0},{2,1},{3,2},{4,3},{5,4},{6,5},{7,6},{8,7},{9,8},{10,9},{11,1... | collective-permute-start | bytes 24584 | tf_op jit(solution)/shard_map/ppermute | solution.py:26
